TPU v7x, 256 devices: a whole 4x4x8 slice. The times are simulated.
256 devices in a mesh: section: 4 (over x), dp: 64 (over y, z, core).
Axes of the slice: x: 4, y: 4, z: 8, core: 2. Of those that a mesh axis runs over, the one named last changes fastest.
Arguments:
- clean_latent: bfloat16 [8192, 1536], P('dp'), may hold values from -60 to 60
- noise_latent: bfloat16 [8192, 1536], P('dp'), may hold values from -6 to 6
- teacher_velocity: bfloat16 [8192, 1536], P('dp'), may hold values from -6 to 6
- step_index: int32 [8192], P('dp'), may hold values from 0 to 3
- modulation: float32 [4, 4, 1536], P('section'), may hold values from -0.6 to 0.6
- up_weight: bfloat16 [4, 36864, 128], P('section', 'dp'), may hold values from -0.21875 to 0.21875
- up_rows: int32 [4, 48, 6], P('section'), may hold values from 0 to 11, as said below
- down_weight: bfloat16 [4, 36864, 128], P('section'), may hold values from -0.109375 to 0.109375
- down_rows: int32 [4, 12, 24], P('section'), may hold values from 0 to 47, as said below
Outputs:
- grad_down: float32 [4, 36864, 128], P('section', 'dp')
Inputs may be any that keep to these rules, and one draw needn't show every extreme that they name: For every section s and hidden block c, up_rows[s, c] holds 6 different feature blocks. For every section s and feature block e, down_rows[s, e] holds 24 different hidden blocks.
All inputs are finite; a program needn't handle non-finite values.
Results may differ from a plain program's by a relative error of at most 0.004.
Values may be sent and summed in bfloat16 or wider, within the bound.
No kernel may reach another device: no remote copies, remote signals or barrier semaphores. Data moves between devices by JAX's collectives and lax.ppermute only.
A program may use at most 128 MiB of HBM per device.

v0:
```python
import math
import jax
import jax.numpy as jnp
from jax import lax
from jax.sharding import PartitionSpec as P

MICRO = 2
EPSILON = 1e-06


def from_behind(block, axis, distance):
    devices = range(lax.axis_size(axis))
    route = [(i - distance, i) for i in devices if i - distance in devices]
    return lax.ppermute(block, axis, route)


def activation(values):
    return jax.nn.gelu(values, approximate=True)


def lookup(step_values, table):
    onehot = (step_values[:, None] == jnp.arange(table.shape[0], dtype=jnp.int32)[None, :]).astype(
        jnp.float32
    )
    return jnp.sum(onehot[:, :, None] * table[None, :, :], axis=1)


def section_forward(stream, scale_rows, up_blocks, up_index, down_blocks, down_index):
    row_count, feature_count = stream.shape
    block_size = up_blocks.shape[-1]
    stream_wide = stream.astype(jnp.float32)
    inverse = lax.rsqrt(jnp.mean(stream_wide * stream_wide, axis=-1, keepdims=True) + EPSILON)
    normed = (stream_wide * inverse * (1.0 + scale_rows)).astype(jnp.bfloat16)
    picked = normed.reshape(row_count, feature_count // block_size, block_size)[:, up_index, :]
    preact = jnp.einsum("rcki,ckij->rcj", picked, up_blocks, preferred_element_type=jnp.float32)
    hidden = activation(preact).astype(jnp.bfloat16)
    gathered = hidden[:, down_index, :]
    mixed_out = jnp.einsum(
        "rekj,ekjf->ref", gathered, down_blocks, preferred_element_type=jnp.float32
    )
    result = (stream_wide + mixed_out.reshape(row_count, feature_count)).astype(jnp.bfloat16)
    return (result, preact.reshape(row_count, -1), hidden.reshape(row_count, -1))


def section_backward(
    cotangent, stream, scale_rows, preact, up_blocks, up_index, down_blocks, down_index
):
    row_count, feature_count = stream.shape
    block_size = up_blocks.shape[-1]
    hidden_count = preact.shape[1]
    grad_blocks = cotangent.reshape(row_count, feature_count // block_size, block_size)
    grad_gathered = jnp.einsum(
        "ref,ekjf->rekj", grad_blocks, down_blocks, preferred_element_type=jnp.float32
    )
    grad_hidden = (
        jnp.zeros((row_count, hidden_count // block_size, block_size), jnp.float32)
        .at[:, down_index, :]
        .add(grad_gathered)
    )
    activated, pullback = jax.vjp(
        activation, preact.reshape(row_count, hidden_count // block_size, block_size)
    )
    grad_preact = pullback(grad_hidden)[0].astype(jnp.bfloat16)
    grad_picked = jnp.einsum(
        "rcj,ckij->rcki", grad_preact, up_blocks, preferred_element_type=jnp.float32
    )
    grad_normed = (
        jnp.zeros((row_count, feature_count // block_size, block_size), jnp.float32)
        .at[:, up_index, :]
        .add(grad_picked)
    )
    grad_normed = grad_normed.reshape(row_count, feature_count)
    stream_wide = stream.astype(jnp.float32)
    inverse = lax.rsqrt(jnp.mean(stream_wide * stream_wide, axis=-1, keepdims=True) + EPSILON)
    scaled = grad_normed * (1.0 + scale_rows)
    grad_stream = inverse * scaled - stream_wide * inverse * inverse * inverse * jnp.mean(
        scaled * stream_wide, axis=-1, keepdims=True
    )
    return (cotangent.astype(jnp.float32) + grad_stream).astype(jnp.bfloat16)


def pick_slot(stack, index):
    return lax.dynamic_index_in_dim(stack, index, 0, keepdims=False)


def store_slot(stack, index, value, valid):
    previous = pick_slot(stack, index)
    return lax.dynamic_update_index_in_dim(stack, jnp.where(valid, value, previous), index, 0)


def per_device(
    clean_latent,
    noise_latent,
    teacher_velocity,
    step_index,
    modulation,
    up_weight,
    up_rows,
    down_weight,
    down_rows,
):
    section_count = lax.axis_size("section")
    section_number = lax.axis_index("section")
    owner_count = lax.axis_size("dp")
    row_total, feature_count = clean_latent.shape
    block_size = up_weight.shape[2]
    hidden_blocks, keep_up = (up_rows.shape[1], up_rows.shape[2])
    width_blocks, keep_down = (down_rows.shape[1], down_rows.shape[2])
    hidden_count = hidden_blocks * block_size
    micro_rows = row_total // MICRO
    turn_count = MICRO + section_count - 1
    loss_scale = 1.0 / math.sqrt(row_total * owner_count)
    gathered_up = lax.all_gather(up_weight, "dp", axis=1, tiled=True)
    up_blocks = gathered_up.reshape(hidden_blocks, keep_up, block_size, block_size)
    up_index = up_rows[0]
    down_blocks = down_weight.reshape(width_blocks, keep_down, block_size, block_size)
    down_index = down_rows[0]
    table = modulation[0]
    fraction = (step_index.astype(jnp.float32) + 1.0) / table.shape[0]
    entry = (
        (1.0 - fraction)[:, None] * clean_latent.astype(jnp.float32)
        + fraction[:, None] * noise_latent.astype(jnp.float32)
    ).astype(jnp.bfloat16)
    entry = entry.reshape(MICRO, micro_rows, feature_count)
    scale_all = lookup(step_index, table).reshape(MICRO, micro_rows, feature_count)
    targets = teacher_velocity.reshape(MICRO, micro_rows, feature_count)

    def forward_turn(turn_index, carry):
        arrived, kept_stream, kept_preact, kept_hidden, kept_grad = carry
        micro_index = turn_index - section_number
        valid = (micro_index >= 0) & (micro_index < MICRO)
        clipped = jnp.clip(micro_index, 0, MICRO - 1)
        stream_in = jnp.where(section_number == 0, pick_slot(entry, clipped), arrived)
        scale_rows = pick_slot(scale_all, clipped)

        def forward_active(operand):
            return section_forward(
                stream_in, scale_rows, up_blocks, up_index, down_blocks, down_index
            )

        def forward_resting(operand):
            return (
                jnp.zeros_like(stream_in),
                jnp.zeros((micro_rows, hidden_count), jnp.float32),
                jnp.zeros((micro_rows, hidden_count), jnp.bfloat16),
            )

        result, preact, hidden = lax.cond(valid, forward_active, forward_resting, 0)
        cotangent = (
            (result.astype(jnp.float32) - pick_slot(targets, clipped).astype(jnp.float32))
            * loss_scale
        ).astype(jnp.bfloat16)
        kept_stream = store_slot(kept_stream, clipped, stream_in, valid)
        kept_preact = store_slot(kept_preact, clipped, preact, valid)
        kept_hidden = store_slot(kept_hidden, clipped, hidden, valid)
        kept_grad = store_slot(
            kept_grad, clipped, cotangent, valid & (section_number == section_count - 1)
        )
        arrived = from_behind(result, "section", 1)
        return (arrived, kept_stream, kept_preact, kept_hidden, kept_grad)

    start = (
        jnp.zeros((micro_rows, feature_count), jnp.bfloat16),
        jnp.zeros((MICRO, micro_rows, feature_count), jnp.bfloat16),
        jnp.zeros((MICRO, micro_rows, hidden_count), jnp.float32),
        jnp.zeros((MICRO, micro_rows, hidden_count), jnp.bfloat16),
        jnp.zeros((MICRO, micro_rows, feature_count), jnp.bfloat16),
    )
    arrived, kept_stream, kept_preact, kept_hidden, kept_grad = lax.fori_loop(
        0, turn_count, forward_turn, start
    )

    def backward_turn(turn_index, carry):
        arrived_grad, kept_cotangent = carry
        micro_index = turn_index - (section_count - 1 - section_number)
        valid = (micro_index >= 0) & (micro_index < MICRO)
        clipped = jnp.clip(micro_index, 0, MICRO - 1)
        incoming = jnp.where(
            section_number == section_count - 1, pick_slot(kept_grad, clipped), arrived_grad
        )

        def backward_active(operand):
            return section_backward(
                incoming,
                pick_slot(kept_stream, clipped),
                pick_slot(scale_all, clipped),
                pick_slot(kept_preact, clipped),
                up_blocks,
                up_index,
                down_blocks,
                down_index,
            )

        def backward_resting(operand):
            return jnp.zeros_like(incoming)

        grad_stream = lax.cond(valid, backward_active, backward_resting, 0)
        kept_cotangent = store_slot(kept_cotangent, clipped, incoming, valid)
        arrived_grad = from_behind(grad_stream, "section", -1)
        return (arrived_grad, kept_cotangent)

    start_back = (
        jnp.zeros((micro_rows, feature_count), jnp.bfloat16),
        jnp.zeros((MICRO, micro_rows, feature_count), jnp.bfloat16),
    )
    arrived_grad, kept_cotangent = lax.fori_loop(0, turn_count, backward_turn, start_back)
    all_rows = MICRO * micro_rows
    hidden_rows = kept_hidden.reshape(all_rows, hidden_count)
    grad_rows_all = kept_cotangent.reshape(all_rows, feature_count)
    packed_rows = width_blocks * keep_down * block_size
    gathered = hidden_rows.reshape(all_rows, hidden_blocks, block_size)[:, down_index, :]
    weight_term = jnp.einsum(
        "tejh,tef->ejhf",
        gathered,
        grad_rows_all.reshape(all_rows, width_blocks, block_size),
        preferred_element_type=jnp.float32,
    )
    grad_down = lax.psum_scatter(
        weight_term.reshape(1, packed_rows, block_size), "dp", scatter_dimension=1, tiled=True
    )
    return grad_down


def solution(mesh):
    in_specs = (
        P("dp", None),
        P("dp", None),
        P("dp", None),
        P("dp"),
        P("section", None, None),
        P("section", "dp", None),
        P("section", None, None),
        P("section", None, None),
        P("section", None, None),
    )
    out_specs = P("section", "dp", None)
    return jax.shard_map(
        per_device, mesh=mesh, in_specs=in_specs, out_specs=out_specs, check_vma=False
    )
```

profile of v0, /device:TPU:4, one launch (start us, length us, event | category | flops | bytes accessed | tf_op | source)
XLA Modules:
  0.0 1123.6 jit_solution(2123157267478633781)
XLA Ops:
  16.2 81.9 %all-gather.2.cloned.1.call-done = bf16[1,36864,128]{2,1,0:T(8,128)(2,1)} async-done(((bf16[1,576,128]{2,1,0:T(8,128)(2,1)}), bf16[1,36864,128]{2,1,0:T(8,128)(2,1)}) %all-gather.2.cloned.1.call-update) | async-done | bytes 9437200 | tf_op jit(solution)/shard_map/all_gather | solution.py:113
  103.1 287.1 %while.39 = (s32[]{:T(128)}, bf16[64,1536]{1,0:T(8,128)(2,1)S(1)}, bf16[2,64,1536]{2,1,0:T(8,128)(2,1)}, f32[2,64,6144]{2,1,0:T(8,128)}, bf16[2,64,6144]{2,1,0:T...) while((s32[]{:T(128)}, bf16[64,1536]{1,0:T(8,128)(2,1)S(1)}, ...), condition=%wide.region_5.6_spmd, body=%wide.region_1.5_spmd.sunk | while | flops 1214156544 | bytes 98133112 | solution.py:169
  134.3 80.9 %collective-permute-done = bf16[64,1536]{1,0:T(8,128)(2,1)S(1)} collective-permute-done((bf16[64,1536]{1,0:T(8,128)(2,1)}, bf16[64,1536]{1,0:T(8,128)(2,1)S(1)}, u32[]{:S(2)}, u32[]{:S(2)}) %collective-permute-start) | collective-permute-done | bytes 196640 | tf_op jit(solution)/shard_map/while/body/eval_jaxpr/ppermute | solution.py:14
  217.8 45.3 %conditional.4 = (bf16[64,1536]{1,0:T(8,128)(2,1)S(1)}, f32[64,6144]{1,0:T(8,128)}, bf16[64,6144]{1,0:T(8,128)(2,1)S(1)}, f32[64,1536]{1,0:T(8,128)}) conditional(s32[]{:T(128)} %convert_element_type.162, () %tuple.92, (bf16[64,1536]{1,0:T(8,128)(2,1)S(1)}, f32[2,64,1536]{2,1,0:T(8,128)}, s32[]{:T(128)}, s32[48,6]{1,0:T(8,128)}, ...), branch_computations={%region_2.2_spmd, %region_3.4_spmd} | conditional | flops 1212681984 | bytes 56843296 | solution.py:148
  220.0 13.3 %gather_fusion = bf16[288,64,128]{2,1,0:T(8,128)(2,1)} fusion(bf16[64,12,128]{2,0,1:T(8,128)(2,1)S(1)} %copy_bitcast_fusion.2, s32[1024]{0:T(1024)S(1)} %pad_clamp_fusion.1), kind=kCustom, calls=%fused_computation | custom fusion | bytes 9438336 | tf_op jit(solution)/shard_map/while/body/eval_jaxpr/cond/branch_1_fun/gather | solution.py:34
  240.5 13.3 %gather_fusion.1 = bf16[288,64,128]{2,1,0:T(8,128)(2,1)} fusion(bf16[64,48,128]{2,0,1:T(8,128)(2,1)S(1)} %get-tuple-element.731, s32[1024]{0:T(1024)S(1)} %pad_clamp_fusion), kind=kCustom, calls=%fused_computation.1 | custom fusion | bytes 9438336 | tf_op jit(solution)/shard_map/while/body/eval_jaxpr/cond/branch_1_fun/gather | solution.py:37
  277.2 45.3 %conditional.4 = (bf16[64,1536]{1,0:T(8,128)(2,1)S(1)}, f32[64,6144]{1,0:T(8,128)}, bf16[64,6144]{1,0:T(8,128)(2,1)S(1)}, f32[64,1536]{1,0:T(8,128)}) conditional(s32[]{:T(128)} %convert_element_type.162, () %tuple.92, (bf16[64,1536]{1,0:T(8,128)(2,1)S(1)}, f32[2,64,1536]{2,1,0:T(8,128)}, s32[]{:T(128)}, s32[48,6]{1,0:T(8,128)}, ...), branch_computations={%region_2.2_spmd, %region_3.4_spmd} | conditional | flops 1212681984 | bytes 56843296 | solution.py:148
  279.4 13.3 %gather_fusion = bf16[288,64,128]{2,1,0:T(8,128)(2,1)} fusion(bf16[64,12,128]{2,0,1:T(8,128)(2,1)S(1)} %copy_bitcast_fusion.2, s32[1024]{0:T(1024)S(1)} %pad_clamp_fusion.1), kind=kCustom, calls=%fused_computation | custom fusion | bytes 9438336 | tf_op jit(solution)/shard_map/while/body/eval_jaxpr/cond/branch_1_fun/gather | solution.py:34
  299.9 13.3 %gather_fusion.1 = bf16[288,64,128]{2,1,0:T(8,128)(2,1)} fusion(bf16[64,48,128]{2,0,1:T(8,128)(2,1)S(1)} %get-tuple-element.731, s32[1024]{0:T(1024)S(1)} %pad_clamp_fusion), kind=kCustom, calls=%fused_computation.1 | custom fusion | bytes 9438336 | tf_op jit(solution)/shard_map/while/body/eval_jaxpr/cond/branch_1_fun/gather | solution.py:37
  339.5 42.7 %collective-permute-start = (bf16[64,1536]{1,0:T(8,128)(2,1)}, bf16[64,1536]{1,0:T(8,128)(2,1)S(1)}, u32[]{:S(2)}, u32[]{:S(2)}) collective-permute-start(bf16[64,1536]{1,0:T(8,128)(2,1)} %copy-done.6), channel_id=1, source_target_pairs={{0,64},{64,128},{128,192},{1,65},{65,129},{129,193},{2,66},{66,130... | collective-permute-start | bytes 589832 | tf_op jit(solution)/shard_map/while/body/eval_jaxpr/ppermute | solution.py:14
  391.0 407.0 %while.40 = (s32[]{:T(128)}, bf16[64,1536]{1,0:T(8,128)(2,1)S(1)}, bf16[2,64,1536]{2,1,0:T(8,128)(2,1)}, s32[]{:T(128)}, pred[]{:T(512)}, /*index=5*/bf16[2,64,1...) while((s32[]{:T(128)}, bf16[64,1536]{1,0:T(8,128)(2,1)S(1)}, ...), condition=%wide.region_13.14_spmd, body=%wide.region_6.13_spmd.sunk | while | flops 1222706944 | bytes 115030680 | solution.py:206
  396.3 92.5 %collective-permute-done.1 = bf16[64,1536]{1,0:T(8,128)(2,1)S(1)} collective-permute-done((bf16[64,1536]{1,0:T(8,128)(2,1)}, bf16[64,1536]{1,0:T(8,128)(2,1)S(1)}, u32[]{:S(2)}, u32[]{:S(2)}) %collective-permute-start.1) | collective-permute-done | bytes 196640 | tf_op jit(solution)/shard_map/while/body/eval_jaxpr/ppermute | solution.py:14
  491.4 89.1 %conditional.5 = (bf16[64,1536]{1,0:T(8,128)(2,1)S(1)}) conditional(s32[]{:T(128)} %convert_element_type.163, () %tuple.96, (bf16[64,1536]{1,0:T(8,128)(2,1)S(1)}, s32[]{:T(128)}, bf16[2,64,1536]{2,1,0:T(8,128)(2,1)}, s32[48,6]{1,0:T(8,128)}, s32[12,24]{1,0:T(8,128)S(1)}, /*index=5*/bf16[12,24,128,128]{3,2,1,0:T(8,128)(2,1)}, ...), branch_computations={%region_7.7_spmd, %region_8.12_spmd} | conditional | flops 1222510336 | bytes 112080184 | solution.py:197
  493.4 10.7 fusion.42
  504.4 29.7 %scatter_fusion = f32[64,48,128]{2,0,1:T(8,128)S(1)} fusion(f32[64,48,128]{2,0,1:T(8,128)S(1)} %broadcast.178, s32[288]{0:T(512)S(1)} %reshape.165, f32[288,64,128]{2,1,0:T(8,128)} %bitcast.172), kind=kCustom, calls=%fused_computation.3 | custom fusion | flops 2359296 | bytes 28312704 | tf_op jit(solution)/shard_map/while/body/eval_jaxpr/cond/branch_1_fun/scatter-add | solution.py:58
  545.8 29.9 %scatter_fusion.1 = f32[64,12,128]{2,0,1:T(8,128)S(1)} fusion(f32[64,12,128]{2,0,1:T(8,128)S(1)} %broadcast.175, s32[288]{0:T(512)S(1)} %reshape.173, f32[288,64,128]{2,1,0:T(8,128)} %bitcast.174), kind=kCustom, calls=%fused_computation.4 | custom fusion | flops 2359296 | bytes 28312704 | tf_op jit(solution)/shard_map/while/body/eval_jaxpr/cond/branch_1_fun/scatter-add | solution.py:70
  591.6 89.1 %conditional.5 = (bf16[64,1536]{1,0:T(8,128)(2,1)S(1)}) conditional(s32[]{:T(128)} %convert_element_type.163, () %tuple.96, (bf16[64,1536]{1,0:T(8,128)(2,1)S(1)}, s32[]{:T(128)}, bf16[2,64,1536]{2,1,0:T(8,128)(2,1)}, s32[48,6]{1,0:T(8,128)}, s32[12,24]{1,0:T(8,128)S(1)}, /*index=5*/bf16[12,24,128,128]{3,2,1,0:T(8,128)(2,1)}, ...), branch_computations={%region_7.7_spmd, %region_8.12_spmd} | conditional | flops 1222510336 | bytes 112080184 | solution.py:197
  593.6 10.7 fusion.42
  604.5 29.7 %scatter_fusion = f32[64,48,128]{2,0,1:T(8,128)S(1)} fusion(f32[64,48,128]{2,0,1:T(8,128)S(1)} %broadcast.178, s32[288]{0:T(512)S(1)} %reshape.165, f32[288,64,128]{2,1,0:T(8,128)} %bitcast.172), kind=kCustom, calls=%fused_computation.3 | custom fusion | flops 2359296 | bytes 28312704 | tf_op jit(solution)/shard_map/while/body/eval_jaxpr/cond/branch_1_fun/scatter-add | solution.py:58
  634.3 10.7 fusion.25
  645.9 29.9 %scatter_fusion.1 = f32[64,12,128]{2,0,1:T(8,128)S(1)} fusion(f32[64,12,128]{2,0,1:T(8,128)S(1)} %broadcast.175, s32[288]{0:T(512)S(1)} %reshape.173, f32[288,64,128]{2,1,0:T(8,128)} %bitcast.174), kind=kCustom, calls=%fused_computation.4 | custom fusion | flops 2359296 | bytes 28312704 | tf_op jit(solution)/shard_map/while/body/eval_jaxpr/cond/branch_1_fun/scatter-add | solution.py:70
  692.4 90.9 %collective-permute-start.1 = (bf16[64,1536]{1,0:T(8,128)(2,1)}, bf16[64,1536]{1,0:T(8,128)(2,1)S(1)}, u32[]{:S(2)}, u32[]{:S(2)}) collective-permute-start(bf16[64,1536]{1,0:T(8,128)(2,1)} %copy-done.7), channel_id=1, source_target_pairs={{64,0},{128,64},{192,128},{65,1},{129,65},{193,129},{66,2},{130,66... | collective-permute-start | bytes 589832 | tf_op jit(solution)/shard_map/while/body/eval_jaxpr/ppermute | solution.py:14
  812.0 12.7 %copy.62 = bf16[12,24,128,128]{2,3,1,0:T(8,128)(2,1)} copy(bf16[12,24,128,128]{3,2,1,0:T(8,128)(2,1)} %bitcast.180) | data formatting | bytes 18874368 | tf_op jit(solution)/shard_map/gather | solution.py:211
  834.9 281.8 %reduce-scatter.2.cloned.1.call-done = f32[1,576,128]{2,1,0:T(8,128)} async-done(((f32[1,36864,128]{2,1,0:T(8,128)}), f32[1,576,128]{2,1,0:T(8,128)}) %reduce-scatter.2.cloned.1.call-update) | async-done | bytes 294928 | tf_op jit(solution)/shard_map/reduce_scatter | solution.py:218
  (267 shorter events, 227.7 us)
Async XLA Ops:
  6.5 91.6 %all-gather.2.cloned.1.call-start = ((), (), s32[]{:S(2)}) async-start(), calls=%async_computation.1 | async-start | bytes 9584640 | tf_op jit(solution)/shard_map/all_gather | solution.py:113
  7.3 1109.5 %reduce-scatter.2.cloned.1.call-start = ((), (), s32[]{:S(2)}) async-start(), calls=%async_computation.2 | async-start | bytes 19169280 | tf_op jit(solution)/shard_map/reduce_scatter | solution.py:218
  108.6 10.3 collective-permute-start
  114.4 2.0 copy-start.1
  115.7 2.0 copy-start.4
  115.7 2.0 copy-start.8
  125.2 90.0 %collective-permute-start = (bf16[64,1536]{1,0:T(8,128)(2,1)}, bf16[64,1536]{1,0:T(8,128)(2,1)S(1)}, u32[]{:S(2)}, u32[]{:S(2)}) collective-permute-start(bf16[64,1536]{1,0:T(8,128)(2,1)} %copy-done.6), channel_id=1, source_target_pairs={{0,64},{64,128},{128,192},{1,65},{65,129},{129,193},{2,66},{66,130... | collective-permute-start | bytes 589832 | tf_op jit(solution)/shard_map/while/body/eval_jaxpr/ppermute | solution.py:14
  129.8 2.0 copy-start.1
  131.2 2.0 copy-start.4
  131.2 2.0 copy-start.8
  134.3 80.9 %copy-start.5 = (bf16[2,64,1536]{2,1,0:T(8,128)(2,1)}, bf16[2,64,1536]{2,1,0:T(8,128)(2,1)S(1)}, u32[]{:S(2)}) copy-start(bf16[2,64,1536]{2,1,0:T(8,128)(2,1)S(1)} %fusion.68) | copy-start | bytes 1179652 | tf_op jit(solution)/shard_map/while
  263.8 10.8 collective-permute-start
  268.4 2.9 copy-start.1
  323.2 10.0 collective-permute-start
  327.8 2.9 copy-start.1
  339.5 49.9 %collective-permute-start = (bf16[64,1536]{1,0:T(8,128)(2,1)}, bf16[64,1536]{1,0:T(8,128)(2,1)S(1)}, u32[]{:S(2)}, u32[]{:S(2)}) collective-permute-start(bf16[64,1536]{1,0:T(8,128)(2,1)} %copy-done.6), channel_id=1, source_target_pairs={{0,64},{64,128},{128,192},{1,65},{65,129},{129,193},{2,66},{66,130... | collective-permute-start | bytes 589832 | tf_op jit(solution)/shard_map/while/body/eval_jaxpr/ppermute | solution.py:14
  384.9 2.0 copy-start.1
  386.2 2.1 copy-start.4
  386.2 2.1 copy-start.8
  394.4 94.4 %collective-permute-start.1 = (bf16[64,1536]{1,0:T(8,128)(2,1)}, bf16[64,1536]{1,0:T(8,128)(2,1)S(1)}, u32[]{:S(2)}, u32[]{:S(2)}) collective-permute-start(bf16[64,1536]{1,0:T(8,128)(2,1)} %copy-done.7), channel_id=1, source_target_pairs={{64,0},{128,64},{192,128},{65,1},{129,65},{193,129},{66,2},{130,66... | collective-permute-start | bytes 589832 | tf_op jit(solution)/shard_map/while/body/eval_jaxpr/ppermute | solution.py:14
  581.2 7.8 collective-permute-start.1
  681.3 7.8 collective-permute-start.1
  692.4 94.4 %collective-permute-start.1 = (bf16[64,1536]{1,0:T(8,128)(2,1)}, bf16[64,1536]{1,0:T(8,128)(2,1)S(1)}, u32[]{:S(2)}, u32[]{:S(2)}) collective-permute-start(bf16[64,1536]{1,0:T(8,128)(2,1)} %copy-done.7), channel_id=1, source_target_pairs={{64,0},{128,64},{192,128},{65,1},{129,65},{193,129},{66,2},{130,66... | collective-permute-start | bytes 589832 | tf_op jit(solution)/shard_map/while/body/eval_jaxpr/ppermute | solution.py:14
  790.2 7.8 collective-permute-start.1
  (34 other events, 37.0 us)
Sparse Core Ops, SparseCore 0:
  10.1 87.9 all-gather.1
  835.1 281.6 reduce-scatter.1
where the time goes:
time: 1130 us; the launch traced here: 1120 us
  waiting for transfers between devices  557 us (49%)
  other arithmetic  176 us (16%)
  starting transfers between devices  152 us (13%)
  local copies, waits for them, and re-layouts  142 us (13%)
  matrix products  81.4 us (7%)
  between operations  13.5 us (1%)
    reduce_scatter x1, waiting for transfers between devices, per_device(): lax.psum_scatter(weight_term.reshape(1, packed_rows, block_size), 'dp', s...  282 us
    ppermute x10, waiting for transfers between devices, from_behind(): return lax.ppermute(block, axis, route)  193 us
    ppermute x10, starting transfers between devices, from_behind(): return lax.ppermute(block, axis, route)  152 us
    all_gather x1, waiting for transfers between devices, per_device(): gathered_up = lax.all_gather(up_weight, 'dp', axis=1, tiled=True)  81.9 us
    scatter-add x2, other arithmetic, section_backward(): grad_normed = jnp.zeros((row_count, feature_count // block_size, block_si...  59.7 us
    scatter-add x2, other arithmetic, section_backward(): grad_hidden = jnp.zeros((row_count, hidden_count // block_size, block_siz...  59.5 us
    dynamic_update_slice x25, other arithmetic, store_slot(): lax.dynamic_update_index_in_dim(stack, jnp.where(valid, value, previous),...  33 us
    gather x2, local copies, waits for them, and re-layouts, section_forward(): gathered = hidden[:, down_index, :]  26.7 us
  transfers between devices with their start and end apart: 12, of which 9 were waited for; matrix products, arithmetic and copies ran while one was open for 3% of the time, Pallas kernels for 0%

commit v1 on v0

--- a/solution.py
+++ b/solution.py
@@ -110,7 +110,9 @@
     micro_rows = row_total // MICRO
     turn_count = MICRO + section_count - 1
     loss_scale = 1.0 / math.sqrt(row_total * owner_count)
-    gathered_up = lax.all_gather(up_weight, "dp", axis=1, tiled=True)
+    gathered_up = jnp.concatenate(
+        lax.all_to_all(jnp.stack([up_weight] * lax.axis_size("dp")), "dp", 0, 0), axis=1
+    )
     up_blocks = gathered_up.reshape(hidden_blocks, keep_up, block_size, block_size)
     up_index = up_rows[0]
     down_blocks = down_weight.reshape(width_blocks, keep_down, block_size, block_size)

time: 1130 us -> 1270 us (1.12)
  waiting for transfers between devices: 557 us -> 679 us
  starting transfers between devices: 152 us -> 165 us
    all_to_all x0 -> x1, waiting for transfers between devices: none -> 204 us  [per_device(): lax.all_to_all(jnp.stack([up_weight] * lax.axis_size('dp')), 'dp', 0, 0)]
    all_gather x1 -> x0, waiting for transfers between devices: 81.9 us -> none  [per_device(): gathered_up = lax.all_gather(up_weight, 'dp', axis=1, tiled=True)]
  transfers between devices with their start and end apart: 12 -> 12, of which waited for: 9 -> 9; matrix products, arithmetic and copies ran while one was open for 3% -> 2% of each run, Pallas kernels for 0% -> 0%
where the time goes in v1:
time: 1270 us; the launch traced here: 1260 us
  waiting for transfers between devices  679 us (53%)
  other arithmetic  172 us (14%)
  starting transfers between devices  165 us (13%)
  local copies, waits for them, and re-layouts  148 us (12%)
  matrix products  81.4 us (6%)
  between operations  13.5 us (1%)
    reduce_scatter x1, waiting for transfers between devices, per_device(): lax.psum_scatter(weight_term.reshape(1, packed_rows, block_size), 'dp', s...  282 us
    all_to_all x1, waiting for transfers between devices, per_device(): lax.all_to_all(jnp.stack([up_weight] * lax.axis_size('dp')), 'dp', 0, 0)  204 us
    ppermute x10, waiting for transfers between devices, from_behind(): return lax.ppermute(block, axis, route)  194 us
    ppermute x10, starting transfers between devices, from_behind(): return lax.ppermute(block, axis, route)  153 us
    scatter-add x2, other arithmetic, section_backward(): grad_normed = jnp.zeros((row_count, feature_count // block_size, block_si...  59.7 us
    scatter-add x2, other arithmetic, section_backward(): grad_hidden = jnp.zeros((row_count, hidden_count // block_size, block_siz...  59.5 us
    dynamic_update_slice x25, other arithmetic, store_slot(): lax.dynamic_update_index_in_dim(stack, jnp.where(valid, value, previous),...  33.1 us
    gather x2, local copies, waits for them, and re-layouts, section_forward(): gathered = hidden[:, down_index, :]  26.7 us
  transfers between devices with their start and end apart: 12, of which 9 were waited for; matrix products, arithmetic and copies ran while one was open for 2% of the time, Pallas kernels for 0%

profile of v1, /device:TPU:4, one launch (start us, length us, event | category | flops | bytes accessed | tf_op | source)
XLA Modules:
  0.0 1259.8 jit_solution(2660246868386327079)
XLA Ops:
  13.4 12.5 all-to-all-start
  29.6 203.7 %all-to-all-done = bf16[64,1,576,128]{3,2,1,0:T(8,128)(2,1)} async-done(((bf16[64,1,576,128]{3,2,1,0:T(8,128)(2,1)}), bf16[64,1,576,128]{3,2,1,0:T(8,128)(2,1)}, u32[]{:S(2)}, u32[]{:S(2)}) %all-to-all-start) | async-done | bytes 9437216 | tf_op jit(solution)/shard_map/all_to_all | solution.py:114
  238.2 287.8 %while.39 = (s32[]{:T(128)}, bf16[64,1536]{1,0:T(8,128)(2,1)S(1)}, bf16[2,64,1536]{2,1,0:T(8,128)(2,1)}, f32[2,64,6144]{2,1,0:T(8,128)}, bf16[2,64,6144]{2,1,0:T...) while((s32[]{:T(128)}, bf16[64,1536]{1,0:T(8,128)(2,1)S(1)}, ...), condition=%wide.region_5.6_spmd, body=%wide.region_1.5_spmd.sunk | while | flops 1214156544 | bytes 98133112 | solution.py:171
  269.6 81.3 %collective-permute-done = bf16[64,1536]{1,0:T(8,128)(2,1)S(1)} collective-permute-done((bf16[64,1536]{1,0:T(8,128)(2,1)}, bf16[64,1536]{1,0:T(8,128)(2,1)S(1)}, u32[]{:S(2)}, u32[]{:S(2)}) %collective-permute-start) | collective-permute-done | bytes 196640 | tf_op jit(solution)/shard_map/while/body/eval_jaxpr/ppermute | solution.py:14
  353.6 45.3 %conditional.4 = (bf16[64,1536]{1,0:T(8,128)(2,1)S(1)}, f32[64,6144]{1,0:T(8,128)}, bf16[64,6144]{1,0:T(8,128)(2,1)S(1)}, f32[64,1536]{1,0:T(8,128)}) conditional(s32[]{:T(128)} %convert_element_type.162, () %tuple.92, (bf16[64,1536]{1,0:T(8,128)(2,1)S(1)}, f32[2,64,1536]{2,1,0:T(8,128)}, s32[]{:T(128)}, s32[48,6]{1,0:T(8,128)}, ...), branch_computations={%region_2.2_spmd, %region_3.4_spmd} | conditional | flops 1212681984 | bytes 56843296 | solution.py:150
  355.7 13.3 %gather_fusion = bf16[288,64,128]{2,1,0:T(8,128)(2,1)} fusion(bf16[64,12,128]{2,0,1:T(8,128)(2,1)S(1)} %copy_bitcast_fusion.2, s32[1024]{0:T(1024)S(1)} %pad_clamp_fusion.1), kind=kCustom, calls=%fused_computation | custom fusion | bytes 9438336 | tf_op jit(solution)/shard_map/while/body/eval_jaxpr/cond/branch_1_fun/gather | solution.py:34
  376.3 13.3 %gather_fusion.1 = bf16[288,64,128]{2,1,0:T(8,128)(2,1)} fusion(bf16[64,48,128]{2,0,1:T(8,128)(2,1)S(1)} %get-tuple-element.731, s32[1024]{0:T(1024)S(1)} %pad_clamp_fusion), kind=kCustom, calls=%fused_computation.1 | custom fusion | bytes 9438336 | tf_op jit(solution)/shard_map/while/body/eval_jaxpr/cond/branch_1_fun/gather | solution.py:37
  412.9 45.2 %conditional.4 = (bf16[64,1536]{1,0:T(8,128)(2,1)S(1)}, f32[64,6144]{1,0:T(8,128)}, bf16[64,6144]{1,0:T(8,128)(2,1)S(1)}, f32[64,1536]{1,0:T(8,128)}) conditional(s32[]{:T(128)} %convert_element_type.162, () %tuple.92, (bf16[64,1536]{1,0:T(8,128)(2,1)S(1)}, f32[2,64,1536]{2,1,0:T(8,128)}, s32[]{:T(128)}, s32[48,6]{1,0:T(8,128)}, ...), branch_computations={%region_2.2_spmd, %region_3.4_spmd} | conditional | flops 1212681984 | bytes 56843296 | solution.py:150
  415.1 13.3 %gather_fusion = bf16[288,64,128]{2,1,0:T(8,128)(2,1)} fusion(bf16[64,12,128]{2,0,1:T(8,128)(2,1)S(1)} %copy_bitcast_fusion.2, s32[1024]{0:T(1024)S(1)} %pad_clamp_fusion.1), kind=kCustom, calls=%fused_computation | custom fusion | bytes 9438336 | tf_op jit(solution)/shard_map/while/body/eval_jaxpr/cond/branch_1_fun/gather | solution.py:34
  435.6 13.3 %gather_fusion.1 = bf16[288,64,128]{2,1,0:T(8,128)(2,1)} fusion(bf16[64,48,128]{2,0,1:T(8,128)(2,1)S(1)} %get-tuple-element.731, s32[1024]{0:T(1024)S(1)} %pad_clamp_fusion), kind=kCustom, calls=%fused_computation.1 | custom fusion | bytes 9438336 | tf_op jit(solution)/shard_map/while/body/eval_jaxpr/cond/branch_1_fun/gather | solution.py:37
  475.1 43.0 %collective-permute-start = (bf16[64,1536]{1,0:T(8,128)(2,1)}, bf16[64,1536]{1,0:T(8,128)(2,1)S(1)}, u32[]{:S(2)}, u32[]{:S(2)}) collective-permute-start(bf16[64,1536]{1,0:T(8,128)(2,1)} %copy-done.6), channel_id=1, source_target_pairs={{0,64},{64,128},{128,192},{1,65},{65,129},{129,193},{2,66},{66,130... | collective-permute-start | bytes 589832 | tf_op jit(solution)/shard_map/while/body/eval_jaxpr/ppermute | solution.py:14
  526.9 407.3 %while.40 = (s32[]{:T(128)}, bf16[64,1536]{1,0:T(8,128)(2,1)S(1)}, bf16[2,64,1536]{2,1,0:T(8,128)(2,1)}, s32[]{:T(128)}, pred[]{:T(512)}, /*index=5*/bf16[2,64,1...) while((s32[]{:T(128)}, bf16[64,1536]{1,0:T(8,128)(2,1)S(1)}, ...), condition=%wide.region_13.14_spmd, body=%wide.region_6.13_spmd.sunk | while | flops 1222706944 | bytes 115030680 | solution.py:208
  532.1 92.9 %collective-permute-done.1 = bf16[64,1536]{1,0:T(8,128)(2,1)S(1)} collective-permute-done((bf16[64,1536]{1,0:T(8,128)(2,1)}, bf16[64,1536]{1,0:T(8,128)(2,1)S(1)}, u32[]{:S(2)}, u32[]{:S(2)}) %collective-permute-start.1) | collective-permute-done | bytes 196640 | tf_op jit(solution)/shard_map/while/body/eval_jaxpr/ppermute | solution.py:14
  627.6 89.0 %conditional.5 = (bf16[64,1536]{1,0:T(8,128)(2,1)S(1)}) conditional(s32[]{:T(128)} %convert_element_type.163, () %tuple.96, (bf16[64,1536]{1,0:T(8,128)(2,1)S(1)}, s32[]{:T(128)}, bf16[2,64,1536]{2,1,0:T(8,128)(2,1)}, s32[48,6]{1,0:T(8,128)}, s32[12,24]{1,0:T(8,128)S(1)}, /*index=5*/bf16[12,24,128,128]{3,2,1,0:T(8,128)(2,1)}, ...), branch_computations={%region_7.7_spmd, %region_8.12_spmd} | conditional | flops 1222510336 | bytes 112080184 | solution.py:199
  629.6 10.7 fusion.42
  640.6 29.7 %scatter_fusion = f32[64,48,128]{2,0,1:T(8,128)S(1)} fusion(f32[64,48,128]{2,0,1:T(8,128)S(1)} %broadcast.181, s32[288]{0:T(512)S(1)} %reshape.164, f32[288,64,128]{2,1,0:T(8,128)} %bitcast.173), kind=kCustom, calls=%fused_computation.3 | custom fusion | flops 2359296 | bytes 28312704 | tf_op jit(solution)/shard_map/while/body/eval_jaxpr/cond/branch_1_fun/scatter-add | solution.py:58
  681.9 29.9 %scatter_fusion.1 = f32[64,12,128]{2,0,1:T(8,128)S(1)} fusion(f32[64,12,128]{2,0,1:T(8,128)S(1)} %broadcast.178, s32[288]{0:T(512)S(1)} %reshape.172, f32[288,64,128]{2,1,0:T(8,128)} %bitcast.174), kind=kCustom, calls=%fused_computation.4 | custom fusion | flops 2359296 | bytes 28312704 | tf_op jit(solution)/shard_map/while/body/eval_jaxpr/cond/branch_1_fun/scatter-add | solution.py:70
  727.8 89.1 %conditional.5 = (bf16[64,1536]{1,0:T(8,128)(2,1)S(1)}) conditional(s32[]{:T(128)} %convert_element_type.163, () %tuple.96, (bf16[64,1536]{1,0:T(8,128)(2,1)S(1)}, s32[]{:T(128)}, bf16[2,64,1536]{2,1,0:T(8,128)(2,1)}, s32[48,6]{1,0:T(8,128)}, s32[12,24]{1,0:T(8,128)S(1)}, /*index=5*/bf16[12,24,128,128]{3,2,1,0:T(8,128)(2,1)}, ...), branch_computations={%region_7.7_spmd, %region_8.12_spmd} | conditional | flops 1222510336 | bytes 112080184 | solution.py:199
  729.7 10.7 fusion.42
  740.7 29.7 %scatter_fusion = f32[64,48,128]{2,0,1:T(8,128)S(1)} fusion(f32[64,48,128]{2,0,1:T(8,128)S(1)} %broadcast.181, s32[288]{0:T(512)S(1)} %reshape.164, f32[288,64,128]{2,1,0:T(8,128)} %bitcast.173), kind=kCustom, calls=%fused_computation.3 | custom fusion | flops 2359296 | bytes 28312704 | tf_op jit(solution)/shard_map/while/body/eval_jaxpr/cond/branch_1_fun/scatter-add | solution.py:58
  782.1 29.9 %scatter_fusion.1 = f32[64,12,128]{2,0,1:T(8,128)S(1)} fusion(f32[64,12,128]{2,0,1:T(8,128)S(1)} %broadcast.178, s32[288]{0:T(512)S(1)} %reshape.172, f32[288,64,128]{2,1,0:T(8,128)} %bitcast.174), kind=kCustom, calls=%fused_computation.4 | custom fusion | flops 2359296 | bytes 28312704 | tf_op jit(solution)/shard_map/while/body/eval_jaxpr/cond/branch_1_fun/scatter-add | solution.py:70
  828.6 90.9 %collective-permute-start.1 = (bf16[64,1536]{1,0:T(8,128)(2,1)}, bf16[64,1536]{1,0:T(8,128)(2,1)S(1)}, u32[]{:S(2)}, u32[]{:S(2)}) collective-permute-start(bf16[64,1536]{1,0:T(8,128)(2,1)} %copy-done.7), channel_id=1, source_target_pairs={{64,0},{128,64},{192,128},{65,1},{129,65},{193,129},{66,2},{130,66... | collective-permute-start | bytes 589832 | tf_op jit(solution)/shard_map/while/body/eval_jaxpr/ppermute | solution.py:14
  948.2 12.7 %copy.79 = bf16[12,24,128,128]{2,3,1,0:T(8,128)(2,1)} copy(bf16[12,24,128,128]{3,2,1,0:T(8,128)(2,1)} %bitcast.180) | data formatting | bytes 18874368 | tf_op jit(solution)/shard_map/gather | solution.py:213
  971.1 281.8 %reduce-scatter.2.cloned.1.call-done = f32[1,576,128]{2,1,0:T(8,128)} async-done(((f32[1,36864,128]{2,1,0:T(8,128)}), f32[1,576,128]{2,1,0:T(8,128)}) %reduce-scatter.2.cloned.1.call-update) | async-done | bytes 294928 | tf_op jit(solution)/shard_map/reduce_scatter | solution.py:220
  (279 shorter events, 238.8 us)
Async XLA Ops:
  13.4 12.6 copy-start.14
  13.4 13.3 %copy-start.13 = (s32[1,12,24]{2,0,1:T(1,128)S(1)}, s32[1,12,24]{2,0,1:T(1,128)}, u32[]{:S(2)}) copy-start(s32[1,12,24]{2,0,1:T(1,128)} %param.25) | copy-start | bytes 3460
  13.4 14.0 %copy-start.15 = (s32[128]{0:T(128)S(1)}, s32[128]{0:T(128)}, u32[]{:S(2)}) copy-start(s32[128]{0:T(128)} %param.20) | copy-start | bytes 1540
  13.4 14.0 %copy-start.12 = (f32[1,4,1536]{2,1,0:T(4,128)S(1)}, f32[1,4,1536]{2,1,0:T(4,128)}, u32[]{:S(2)}) copy-start(f32[1,4,1536]{2,1,0:T(4,128)} %param.21) | copy-start | bytes 73732
  13.4 15.2 %copy-start.9 = (bf16[128,1536]{1,0:T(8,128)(2,1)S(1)}, bf16[128,1536]{1,0:T(8,128)(2,1)}, u32[]{:S(2)}) copy-start(bf16[128,1536]{1,0:T(8,128)(2,1)} %param.18) | copy-start | bytes 1179652
  13.4 15.2 %copy-start.10 = (bf16[128,1536]{1,0:T(8,128)(2,1)S(1)}, bf16[128,1536]{1,0:T(8,128)(2,1)}, u32[]{:S(2)}) copy-start(bf16[128,1536]{1,0:T(8,128)(2,1)} %param.17) | copy-start | bytes 1179652
  13.4 219.8 %all-to-all-start = ((bf16[64,1,576,128]{3,2,1,0:T(8,128)(2,1)}), bf16[64,1,576,128]{3,2,1,0:T(8,128)(2,1)}, u32[]{:S(2)}, u32[]{:S(2)}) async-start(bf16[64,1,576,128]{3,2,1,0:T(8,128)(2,1)} %stack.2), calls=%async_computation | async-start | bytes 18874368 | tf_op jit(solution)/shard_map/all_to_all | solution.py:114
  25.9 1227.0 %reduce-scatter.2.cloned.1.call-start = ((), (), s32[]{:S(2)}) async-start(), calls=%async_computation.2 | async-start | bytes 19169280 | tf_op jit(solution)/shard_map/reduce_scatter | solution.py:220
  243.9 10.3 collective-permute-start
  251.1 2.0 copy-start.8
  260.4 90.5 %collective-permute-start = (bf16[64,1536]{1,0:T(8,128)(2,1)}, bf16[64,1536]{1,0:T(8,128)(2,1)S(1)}, u32[]{:S(2)}, u32[]{:S(2)}) collective-permute-start(bf16[64,1536]{1,0:T(8,128)(2,1)} %copy-done.6), channel_id=1, source_target_pairs={{0,64},{64,128},{128,192},{1,65},{65,129},{129,193},{2,66},{66,130... | collective-permute-start | bytes 589832 | tf_op jit(solution)/shard_map/while/body/eval_jaxpr/ppermute | solution.py:14
  269.6 81.3 %copy-start.5 = (bf16[2,64,1536]{2,1,0:T(8,128)(2,1)}, bf16[2,64,1536]{2,1,0:T(8,128)(2,1)S(1)}, u32[]{:S(2)}) copy-start(bf16[2,64,1536]{2,1,0:T(8,128)(2,1)S(1)} %fusion.68) | copy-start | bytes 1179652 | tf_op jit(solution)/shard_map/while
  399.5 10.8 collective-permute-start
  404.1 2.9 copy-start.1
  458.8 10.0 collective-permute-start
  463.5 2.9 copy-start.1
  475.1 50.2 %collective-permute-start = (bf16[64,1536]{1,0:T(8,128)(2,1)}, bf16[64,1536]{1,0:T(8,128)(2,1)S(1)}, u32[]{:S(2)}, u32[]{:S(2)}) collective-permute-start(bf16[64,1536]{1,0:T(8,128)(2,1)} %copy-done.6), channel_id=1, source_target_pairs={{0,64},{64,128},{128,192},{1,65},{65,129},{129,193},{2,66},{66,130... | collective-permute-start | bytes 589832 | tf_op jit(solution)/shard_map/while/body/eval_jaxpr/ppermute | solution.py:14
  522.2 2.1 copy-start.4
  522.2 2.1 copy-start.8
  530.2 94.8 %collective-permute-start.1 = (bf16[64,1536]{1,0:T(8,128)(2,1)}, bf16[64,1536]{1,0:T(8,128)(2,1)S(1)}, u32[]{:S(2)}, u32[]{:S(2)}) collective-permute-start(bf16[64,1536]{1,0:T(8,128)(2,1)} %copy-done.7), channel_id=1, source_target_pairs={{64,0},{128,64},{192,128},{65,1},{129,65},{193,129},{66,2},{130,66... | collective-permute-start | bytes 589832 | tf_op jit(solution)/shard_map/while/body/eval_jaxpr/ppermute | solution.py:14
  717.4 7.8 collective-permute-start.1
  817.5 7.8 collective-permute-start.1
  828.6 94.4 %collective-permute-start.1 = (bf16[64,1536]{1,0:T(8,128)(2,1)}, bf16[64,1536]{1,0:T(8,128)(2,1)S(1)}, u32[]{:S(2)}, u32[]{:S(2)}) collective-permute-start(bf16[64,1536]{1,0:T(8,128)(2,1)} %copy-done.7), channel_id=1, source_target_pairs={{64,0},{128,64},{192,128},{65,1},{129,65},{193,129},{66,2},{130,66... | collective-permute-start | bytes 589832 | tf_op jit(solution)/shard_map/while/body/eval_jaxpr/ppermute | solution.py:14
  926.4 7.8 collective-permute-start.1
  (40 other events, 49.0 us)
Sparse Core Ops, SparseCore 0:
  971.2 281.6 reduce-scatter.1
